TPU v7x, 512 devices: a whole 4x8x8 slice. The times are simulated.
512 devices in a mesh: band: 64 (over y, z), lev: 8 (over x, core).
Axes of the slice: x: 4, y: 8, z: 8, core: 2. Of those that a mesh axis runs over, the one named last changes fastest.
Arguments:
- concentration: float32 [4, 8, 128, 256], P(None, 'lev', 'band'), may hold values from 0.1 to 2
- target: float32 [4, 8, 128, 256], P(None, 'lev', 'band'), may hold values from -6 to 6
- zonal_wind: float32 [8, 128, 256], P('lev', 'band'), may hold values from -0.6 to 0.6
- merid_wind: float32 [8, 128, 256], P('lev', 'band'), may hold values from -0.6 to 0.6
- sea_mask: int32 [128, 256], P('band'), may hold values 0 or 1
- first_weight: float32 [2, 20, 128], replicated, may hold values from -1.25 to 1.25
- first_bias: float32 [2, 128], replicated, may hold values from -3 to 3
- middle_weight: float32 [2, 128, 128], replicated, may hold values from -0.5 to 0.5
- middle_bias: float32 [2, 128], replicated, may hold values from -3 to 3
- last_weight: float32 [2, 4, 128], replicated, may hold values from -0.125 to 0.125
- last_bias: float32 [2, 4], replicated, may hold values from -0.6 to 0.6
Outputs:
- final_field: float32 [4, 8, 128, 256], P(None, 'lev', 'band')
- first_weight_grad: float32 [2, 20, 128], replicated
- first_bias_grad: float32 [2, 128], replicated
- middle_weight_grad: float32 [2, 128, 128], replicated
- middle_bias_grad: float32 [2, 128], replicated
- last_weight_grad: float32 [2, 4, 128], replicated
- last_bias_grad: float32 [2, 4], replicated
Inputs may be any that keep to these rules, and one draw needn't show every extreme that they name: `sea_mask`: 1 marks a sea cell, 0 a land cell.
All inputs are finite; a program needn't handle non-finite values. No bound on the sum of `sea_mask` on one device may be relied on, other than what follows from the above.
Results may differ from a plain program's by a relative error of at most 0.00013.
Values sent between devices are 32-bit elements; how exact they have to be, the bound alone decides.
A program may use at most 64 MiB of HBM per device.

v0:
```python
import math
import jax
import jax.numpy as jnp
from jax import lax
from jax.sharding import PartitionSpec as P

STEPS = 3
stencil_base = (-1.0 / 12.0, 7.0 / 12.0, 7.0 / 12.0, -1.0 / 12.0)


def cut_along(array, direction, start, length):
    return lax.slice_in_dim(array, start, start + length, axis=direction)


def pad_along(array, direction, width):
    widths = [(0, 0)] * array.ndim
    widths[direction] = (width, width)
    return jnp.pad(array, widths)


def face_flux(network, stencil, courant, mask_low, mask_high):
    w_first, b_first, w_second, b_second, w_last, b_last = network
    face_shape = courant.shape
    columns = courant.size
    nbins = stencil.shape[1]
    features = jnp.concatenate(
        [
            stencil.reshape(4 * nbins, columns),
            courant.reshape(1, columns),
            (courant * courant).reshape(1, columns),
            mask_low.reshape(1, columns),
            mask_high.reshape(1, columns),
        ],
        0,
    )
    hidden_one = jnp.tanh(
        jnp.dot(w_first.T, features, precision=lax.Precision.HIGHEST) + b_first[:, None]
    )
    hidden_two = jnp.tanh(
        jnp.dot(w_second.T, hidden_one, precision=lax.Precision.HIGHEST) + b_second[:, None]
    )
    output = jnp.dot(w_last, hidden_two, precision=lax.Precision.HIGHEST) + b_last[:, None]
    correction = output - jnp.mean(output, 0, keepdims=True)
    weights_face = jnp.asarray(stencil_base, jnp.float32)[:, None] + correction
    face_value = jnp.sum(weights_face.reshape((4, 1) + face_shape) * stencil, 0)
    return courant[None] * face_value


def advance(network, padded, wind_padded, mask_padded, direction):
    length = padded.shape[direction] - 4
    stencil = jnp.stack([cut_along(padded, direction, offset, length + 1) for offset in range(4)])
    courant = 0.5 * (
        cut_along(wind_padded, direction - 1, 0, length + 1)
        + cut_along(wind_padded, direction - 1, 1, length + 1)
    )
    mask_low = cut_along(mask_padded, direction - 1, 0, length + 1)
    mask_high = cut_along(mask_padded, direction - 1, 1, length + 1)
    fluxes = face_flux(network, stencil, courant, mask_low, mask_high)
    centre = cut_along(padded, direction, 2, length)
    return centre - (
        cut_along(fluxes, direction, 1, length) - cut_along(fluxes, direction, 0, length)
    )


def to_columns(field):
    return lax.all_to_all(field, "band", split_axis=3, concat_axis=2, tiled=True)


def to_rows(field):
    return lax.all_to_all(field, "band", split_axis=2, concat_axis=3, tiled=True)


def on_device(
    concentration,
    target,
    zonal_wind,
    merid_wind,
    sea_mask,
    first_weight,
    first_bias,
    middle_weight,
    middle_bias,
    last_weight,
    last_bias,
):
    params = (first_weight, first_bias, middle_weight, middle_bias, last_weight, last_bias)
    zonal_net = tuple((member[0] for member in params))
    merid_net = tuple((member[1] for member in params))
    bins_here, levels_here, row_count, col_count = concentration.shape
    total_cells = (
        bins_here
        * levels_here
        * row_count
        * col_count
        * lax.axis_size("band")
        * lax.axis_size("lev")
    )
    loss_scale = 1.0 / math.sqrt(total_cells)
    sea_field = sea_mask.astype(jnp.float32)[None]
    wind_zonal = pad_along(zonal_wind, 2, 1)
    mask_zonal = pad_along(sea_field, 2, 1)
    stacked = jnp.concatenate([merid_wind, sea_field], 0)
    columns_data = lax.all_to_all(stacked, "band", split_axis=2, concat_axis=1, tiled=True)
    wind_merid = pad_along(columns_data[:levels_here], 1, 1)
    mask_merid = pad_along(columns_data[levels_here:], 1, 1)

    def zonal_sweep(network, padded):
        return advance(network, padded, wind_zonal, mask_zonal, 3)

    def merid_sweep(network, padded):
        return advance(network, padded, wind_merid, mask_merid, 2)

    pullbacks = []
    field = concentration
    for step_number in range(STEPS):
        field, zonal_back = jax.vjp(zonal_sweep, zonal_net, pad_along(field, 3, 2))
        moved, merid_back = jax.vjp(merid_sweep, merid_net, pad_along(to_columns(field), 2, 2))
        field = to_rows(moved)
        pullbacks.append((zonal_back, merid_back))
    cotangent = (field - target) * loss_scale
    sums = tuple((jnp.zeros_like(member) for member in params))
    for step_number in reversed(range(STEPS)):
        zonal_back, merid_back = pullbacks[step_number]
        merid_grads, padded_grad = merid_back(to_columns(cotangent))
        cotangent = to_rows(padded_grad[:, :, 2:-2])
        zonal_grads, padded_grad = zonal_back(cotangent)
        cotangent = padded_grad[:, :, :, 2:-2]
        step_grads = tuple(
            (
                jnp.stack([zonal_part, merid_part])
                for zonal_part, merid_part in zip(zonal_grads, merid_grads)
            )
        )
        sums = tuple((earlier + latest for earlier, latest in zip(sums, step_grads)))
    sums = lax.psum((sums[0], sums[1], sums[2], sums[3], sums[4], sums[5]), ("band", "lev"))
    return (field, sums[0], sums[1], sums[2], sums[3], sums[4], sums[5])


def solution(mesh):
    return jax.shard_map(
        on_device,
        mesh=mesh,
        in_specs=(
            P(None, "lev", "band", None),
            P(None, "lev", "band", None),
            P("lev", "band", None),
            P("lev", "band", None),
            P("band", None),
            P(),
            P(),
            P(),
            P(),
            P(),
            P(),
        ),
        out_specs=(P(None, "lev", "band", None), P(), P(), P(), P(), P(), P()),
        check_vma=False,
    )
```

profile of v0, /device:TPU:1, one launch (start us, length us, event | category | flops | bytes accessed | tf_op | source)
XLA Modules:
  0.0 649.2 jit_solution(2578516520645093349)
XLA Ops:
  9.5 17.3 %all-to-all-start.1 = ((f32[2,2,256]{1,0,2:T(2,128)}), f32[2,2,256]{1,0,2:T(2,128)S(1)}, u32[]{:S(2)}, u32[]{:S(2)}) async-start(f32[2,2,256]{1,0,2:T(2,128)} %copy.634), calls=%async_computation.1 | async-start | bytes 524288 | tf_op jit(solution)/shard_map/all_to_all | solution.py:103
  36.5 3.0 all-to-all-done.1
  39.6 9.1 %all-to-all-start = ((f32[4,1,2,256]{0,2,1,3:T(2,128)}), f32[4,1,2,256]{0,2,1,3:T(2,128)S(1)}, u32[]{:S(2)}, u32[]{:S(2)}) async-start(f32[4,1,2,256]{0,2,1,3:T(2,128)} %copy.631), calls=%async_computation | async-start | bytes 524288 | tf_op jit(solution)/shard_map/all_to_all | solution.py:66
  50.4 10.8 %all-to-all-done = f32[4,1,2,256]{0,2,1,3:T(2,128)S(1)} async-done(((f32[4,1,2,256]{0,2,1,3:T(2,128)}), f32[4,1,2,256]{0,2,1,3:T(2,128)S(1)}, u32[]{:S(2)}, u32[]{:S(2)}) %all-to-all-start) | async-done | bytes 8224 | tf_op jit(solution)/shard_map/all_to_all | solution.py:66
  66.5 18.4 %all_to_all.231 = f32[4,1,128,4]{3,0,1,2:T(4,128)S(1)} all-to-all(f32[4,1,128,4]{3,0,1,2:T(4,128)S(1)} %copy.642), channel_id=1, replica_groups=mesh['band'=64,'lev'=8] {'band'}, dimensions={2} | all-to-all | bytes 16384 | tf_op jit(solution)/shard_map/all_to_all | solution.py:70
  88.9 18.4 %all_to_all.232 = f32[4,1,2,256]{0,2,1,3:T(2,128)S(1)} all-to-all(f32[4,1,2,256]{0,2,1,3:T(2,128)S(1)} %copy.646), channel_id=1, replica_groups=mesh['band'=64,'lev'=8] {'band'}, dimensions={3} | all-to-all | bytes 16384 | tf_op jit(solution)/shard_map/all_to_all | solution.py:66
  110.4 1.5 concatenate.121
  111.9 1.3 fusion.8
  117.3 18.4 %all_to_all.233 = f32[4,1,128,4]{3,0,1,2:T(4,128)S(1)} all-to-all(f32[4,1,128,4]{3,0,1,2:T(4,128)S(1)} %copy.651), channel_id=1, replica_groups=mesh['band'=64,'lev'=8] {'band'}, dimensions={2} | all-to-all | bytes 16384 | tf_op jit(solution)/shard_map/all_to_all | solution.py:70
  139.6 18.4 %all_to_all.234 = f32[4,1,2,256]{0,2,1,3:T(2,128)S(1)} all-to-all(f32[4,1,2,256]{0,2,1,3:T(2,128)S(1)} %copy.655), channel_id=1, replica_groups=mesh['band'=64,'lev'=8] {'band'}, dimensions={3} | all-to-all | bytes 16384 | tf_op jit(solution)/shard_map/all_to_all | solution.py:66
  160.7 1.5 slice_bitcast_fusion.15
  163.3 2.2 reshape.1580
  165.5 2.7 concatenate.123
  168.2 1.5 fusion.6
  172.7 1.3 add_bitcast_fusion
  174.0 1.6 mul.546
  175.5 1.9 multiply_reduce_fusion
  177.4 1.7 copy.716
  179.9 1.4 fusion.44
  181.2 1.6 copy.660
  182.8 18.8 %all_to_all.235 = f32[4,1,128,4]{3,0,1,2:T(4,128)S(1)} all-to-all(f32[4,1,128,4]{3,0,1,2:T(4,128)} %copy.660), channel_id=1, replica_groups=mesh['band'=64,'lev'=8] {'band'}, dimensions={2} | all-to-all | bytes 16384 | tf_op jit(solution)/shard_map/all_to_all | solution.py:70
  202.4 1.7 all_to_all.193
  205.5 1.6 copy.664
  207.0 18.1 %all_to_all.236 = f32[4,1,2,256]{0,2,1,3:T(2,128)} all-to-all(f32[4,1,2,256]{0,2,1,3:T(2,128)} %copy.664), channel_id=1, replica_groups=mesh['band'=64,'lev'=8] {'band'}, dimensions={3} | all-to-all | bytes 16384 | tf_op jit(solution)/shard_map/all_to_all | solution.py:66
  225.2 2.6 copy.711
  227.8 1.9 copy.666
  229.7 1.7 copy.667
  232.0 1.4 multiply_bitcast_fusion.2
  233.4 1.6 copy.669
  235.0 1.9 multiply_reduce_fusion.7
  237.6 1.7 reshape.1587
  239.3 1.6 fusion.90
  242.2 1.3 convolution_bitcast_fusion.4
  250.9 4.7 all-to-all-start.8
  255.6 1.5 convolution_bitcast_fusion.21
  257.2 11.0 %all-to-all-done.8 = f32[4,1,128,4]{3,0,1,2:T(4,128)S(1)} async-done(((f32[4,1,128,4]{3,0,1,2:T(4,128)}), f32[4,1,128,4]{3,0,1,2:T(4,128)S(1)}, u32[]{:S(2)}, u32[]{:S(2)}) %all-to-all-start.8) | async-done | bytes 8224 | tf_op jit(solution)/shard_map/all_to_all | solution.py:70
  275.7 5.0 all-to-all-start.9
  281.5 11.8 %all-to-all-done.9 = f32[4,1,2,256]{0,2,1,3:T(2,128)S(1)} async-done(((f32[4,1,2,256]{0,2,1,3:T(2,128)}), f32[4,1,2,256]{0,2,1,3:T(2,128)S(1)}, u32[]{:S(2)}, u32[]{:S(2)}) %all-to-all-start.9) | async-done | bytes 8224 | tf_op jit(solution)/shard_map/all_to_all | solution.py:66
  299.1 1.3 convolution_bitcast_fusion.2
  305.4 4.7 all-to-all-start.10
  310.4 12.3 %all-to-all-done.10 = f32[4,1,128,4]{3,0,1,2:T(4,128)S(1)} async-done(((f32[4,1,128,4]{3,0,1,2:T(4,128)}), f32[4,1,128,4]{3,0,1,2:T(4,128)S(1)}, u32[]{:S(2)}, u32[]{:S(2)}) %all-to-all-start.10) | async-done | bytes 8224 | tf_op jit(solution)/shard_map/all_to_all | solution.py:70
  327.3 4.8 all-to-all-start.11
  332.3 12.3 %all-to-all-done.11 = f32[4,1,2,256]{0,2,1,3:T(2,128)S(1)} async-done(((f32[4,1,2,256]{0,2,1,3:T(2,128)}), f32[4,1,2,256]{0,2,1,3:T(2,128)S(1)}, u32[]{:S(2)}, u32[]{:S(2)}) %all-to-all-start.11) | async-done | bytes 8224 | tf_op jit(solution)/shard_map/all_to_all | solution.py:66
  351.7 4.7 all-to-all-start.12
  356.7 12.2 %all-to-all-done.12 = f32[4,1,128,4]{3,0,1,2:T(4,128)S(1)} async-done(((f32[4,1,128,4]{3,0,1,2:T(4,128)}), f32[4,1,128,4]{3,0,1,2:T(4,128)S(1)}, u32[]{:S(2)}, u32[]{:S(2)}) %all-to-all-start.12) | async-done | bytes 8224 | tf_op jit(solution)/shard_map/all_to_all | solution.py:70
  373.4 104.7 %all-reduce.47 = (f32[2,20,128]{2,1,0:T(8,128)S(1)}, f32[2,128]{1,0:T(2,128)}, f32[2,128]{1,0:T(2,128)}, f32[2,4,128]{2,1,0:T(4,128)}, f32[2,4]{1,0:T(2,128)}) all-reduce(f32[2,20,128]{2,1,0:T(8,128)S(1)} %fusion.37, f32[2,128]{1,0:T(2,128)S(1)} %get-tuple-element.216, ...), channel_id=1, replica_groups=mesh['band'=64,'lev'=8] {'band','lev'}, use_global_device_ids=true, to_apply=%region_24.25 | all-reduce | flops 6664 | bytes 53312 | tf_op jit(solution)/shard_map/psum | solution.py:135
  478.7 161.8 %all-reduce.50.cloned.1.call-done = f32[2,128,128]{2,1,0:T(8,128)} async-done(((f32[2,128,128]{2,1,0:T(8,128)}), f32[2,128,128]{2,1,0:T(8,128)}) %all-reduce.50.cloned.1.call-update) | async-done | bytes 131088 | tf_op jit(solution)/shard_map/psum | solution.py:135
  640.6 1.6 copy.764
  (493 shorter events, 88.1 us)
Async XLA Ops:
  7.2 26.5 %copy-start = (f32[2,128,128]{2,1,0:T(8,128)S(1)}, f32[2,128,128]{2,1,0:T(8,128)}, u32[]{:S(2)}) copy-start(f32[2,128,128]{2,1,0:T(8,128)} %param.24) | copy-start | bytes 393220
  8.6 26.4 %copy-start.73 = (f32[2,4,128]{2,1,0:T(4,128)S(1)}, f32[2,4,128]{2,1,0:T(4,128)}, u32[]{:S(2)}) copy-start(f32[2,4,128]{2,1,0:T(4,128)} %param.26) | copy-start | bytes 12292
  9.5 25.9 %copy-start.100 = (f32[4]{0:T(128)S(1)}, f32[4]{0:T(128)}, u32[]{:S(2)}) copy-start(f32[4]{0:T(128)} %constant.29.clone) | copy-start | bytes 52
  9.5 26.1 %copy-start.82 = (f32[4,1,2,256]{3,2,1,0:T(2,128)S(1)}, f32[4,1,2,256]{3,2,1,0:T(2,128)}, u32[]{:S(2)}) copy-start(f32[4,1,2,256]{3,2,1,0:T(2,128)} %param.17) | copy-start | bytes 24580
  9.5 30.1 %all-to-all-start.1 = ((f32[2,2,256]{1,0,2:T(2,128)}), f32[2,2,256]{1,0,2:T(2,128)S(1)}, u32[]{:S(2)}, u32[]{:S(2)}) async-start(f32[2,2,256]{1,0,2:T(2,128)} %copy.634), calls=%async_computation.1 | async-start | bytes 524288 | tf_op jit(solution)/shard_map/all_to_all | solution.py:103
  29.1 34.0 %copy-start.103 = (f32[128]{0:T(128)}, f32[128]{0:T(128)S(1)}, u32[]{:S(2)}) copy-start(f32[128]{0:T(128)S(1)} %get-tuple-element.178) | copy-start | bytes 1540
  29.1 56.4 %copy-start.105 = (f32[128]{0:T(128)}, f32[128]{0:T(128)S(1)}, u32[]{:S(2)}) copy-start(f32[128]{0:T(128)S(1)} %get-tuple-element.179) | copy-start | bytes 1540
  29.9 34.0 %copy-start.111 = (f32[128]{0:T(128)}, f32[128]{0:T(128)S(1)}, u32[]{:S(2)}) copy-start(f32[128]{0:T(128)S(1)} %get-tuple-element.176) | copy-start | bytes 1540
  29.9 56.3 %copy-start.112 = (f32[128]{0:T(128)}, f32[128]{0:T(128)S(1)}, u32[]{:S(2)}) copy-start(f32[128]{0:T(128)S(1)} %get-tuple-element.177) | copy-start | bytes 1540
  30.6 33.8 %copy-start.104 = (f32[4]{0:T(128)}, f32[4]{0:T(128)S(1)}, u32[]{:S(2)}) copy-start(f32[4]{0:T(128)S(1)} %get-tuple-element.174) | copy-start | bytes 52
  30.6 56.1 %copy-start.107 = (f32[4]{0:T(128)}, f32[4]{0:T(128)S(1)}, u32[]{:S(2)}) copy-start(f32[4]{0:T(128)S(1)} %get-tuple-element.175) | copy-start | bytes 52
  30.7 54.7 %copy-start.91 = (f32[1,514]{1,0:T(1,128)}, f32[1,514]{1,0:T(1,128)S(1)}, u32[]{:S(2)}) copy-start(f32[1,514]{1,0:T(1,128)S(1)} %reshape.1571) | copy-start | bytes 6172
  30.8 54.6 %copy-start.93 = (f32[1,514]{1,0:T(1,128)}, f32[1,514]{1,0:T(1,128)S(1)}, u32[]{:S(2)}) copy-start(f32[1,514]{1,0:T(1,128)S(1)} %reshape.1570) | copy-start | bytes 6172
  31.7 53.7 %copy-start.95 = (f32[1,514]{1,0:T(1,128)}, f32[1,514]{1,0:T(1,128)S(1)}, u32[]{:S(2)}) copy-start(f32[1,514]{1,0:T(1,128)S(1)} %reshape.1569) | copy-start | bytes 6172
  31.8 53.6 %copy-start.97 = (f32[1,514]{1,0:T(1,128)}, f32[1,514]{1,0:T(1,128)S(1)}, u32[]{:S(2)}) copy-start(f32[1,514]{1,0:T(1,128)S(1)} %reshape.1568) | copy-start | bytes 6172
  32.7 52.8 %copy-start.43 = (f32[1,20,128]{2,0,1:T(1,128)}, f32[1,20,128]{2,0,1:T(1,128)S(1)}, u32[]{:S(2)}) copy-start(f32[1,20,128]{2,0,1:T(1,128)S(1)} %get-tuple-element.154) | copy-start | bytes 30724
  39.6 21.6 %all-to-all-start = ((f32[4,1,2,256]{0,2,1,3:T(2,128)}), f32[4,1,2,256]{0,2,1,3:T(2,128)S(1)}, u32[]{:S(2)}, u32[]{:S(2)}) async-start(f32[4,1,2,256]{0,2,1,3:T(2,128)} %copy.631), calls=%async_computation | async-start | bytes 524288 | tf_op jit(solution)/shard_map/all_to_all | solution.py:66
  116.6 19.5 %copy-start.92 = (f32[1,514]{1,0:T(1,128)S(1)}, f32[1,514]{1,0:T(1,128)}, u32[]{:S(2)}) copy-start(f32[1,514]{1,0:T(1,128)} %copy-done.91) | copy-start | bytes 6172
  116.6 19.5 %copy-start.94 = (f32[1,514]{1,0:T(1,128)S(1)}, f32[1,514]{1,0:T(1,128)}, u32[]{:S(2)}) copy-start(f32[1,514]{1,0:T(1,128)} %copy-done.93) | copy-start | bytes 6172
  116.7 19.5 %copy-start.96 = (f32[1,514]{1,0:T(1,128)S(1)}, f32[1,514]{1,0:T(1,128)}, u32[]{:S(2)}) copy-start(f32[1,514]{1,0:T(1,128)} %copy-done.95) | copy-start | bytes 6172
  116.7 19.5 %copy-start.98 = (f32[1,514]{1,0:T(1,128)S(1)}, f32[1,514]{1,0:T(1,128)}, u32[]{:S(2)}) copy-start(f32[1,514]{1,0:T(1,128)} %copy-done.97) | copy-start | bytes 6172
  116.7 19.5 %copy-start.44 = (f32[1,20,128]{2,0,1:T(1,128)S(1)}, f32[1,20,128]{2,0,1:T(1,128)}, u32[]{:S(2)}) copy-start(f32[1,20,128]{2,0,1:T(1,128)} %copy-done.43) | copy-start | bytes 30724
  116.7 19.5 %copy-start.106 = (f32[128]{0:T(128)S(1)}, f32[128]{0:T(128)}, u32[]{:S(2)}) copy-start(f32[128]{0:T(128)} %copy-done.105) | copy-start | bytes 1540
  117.1 19.8 %copy-start.113 = (f32[128]{0:T(128)S(1)}, f32[128]{0:T(128)}, u32[]{:S(2)}) copy-start(f32[128]{0:T(128)} %copy-done.112) | copy-start | bytes 1540
  249.9 18.6 %copy-start.66 = (f32[1,4,1,2,257]{4,3,1,2,0:T(2,128)S(1)}, f32[1,4,1,2,257]{4,3,1,2,0:T(2,128)}, u32[]{:S(2)}) copy-start(f32[1,4,1,2,257]{4,3,1,2,0:T(2,128)} %copy-done.65) | copy-start | bytes 24676
  249.9 18.6 %copy-start.68 = (f32[1,4,1,2,257]{4,3,1,2,0:T(2,128)S(1)}, f32[1,4,1,2,257]{4,3,1,2,0:T(2,128)}, u32[]{:S(2)}) copy-start(f32[1,4,1,2,257]{4,3,1,2,0:T(2,128)} %copy-done.67) | copy-start | bytes 24676
  249.9 18.6 %copy-start.70 = (f32[1,4,1,2,257]{4,3,1,2,0:T(2,128)S(1)}, f32[1,4,1,2,257]{4,3,1,2,0:T(2,128)}, u32[]{:S(2)}) copy-start(f32[1,4,1,2,257]{4,3,1,2,0:T(2,128)} %copy-done.69) | copy-start | bytes 24676
  250.0 18.6 %copy-start.72 = (f32[1,4,1,2,257]{4,3,1,2,0:T(2,128)S(1)}, f32[1,4,1,2,257]{4,3,1,2,0:T(2,128)}, u32[]{:S(2)}) copy-start(f32[1,4,1,2,257]{4,3,1,2,0:T(2,128)} %copy-done.71) | copy-start | bytes 24676
  250.0 19.6 %copy-start.10 = (f32[514,128]{1,0:T(8,128)S(1)}, f32[514,128]{1,0:T(8,128)}, u32[]{:S(2)}) copy-start(f32[514,128]{1,0:T(8,128)} %copy-done.9) | copy-start | bytes 789508
  250.0 19.6 %copy-start.76 = (f32[2,4,128]{2,1,0:T(4,128)S(1)}, f32[2,4,128]{2,1,0:T(4,128)}, u32[]{:S(2)}) copy-start(f32[2,4,128]{2,1,0:T(4,128)} %param.26) | copy-start | bytes 12292
  250.9 19.9 %copy-start.23 = (f32[514,128]{1,0:T(8,128)S(1)}, f32[514,128]{1,0:T(8,128)}, u32[]{:S(2)}) copy-start(f32[514,128]{1,0:T(8,128)} %copy-done.22) | copy-start | bytes 789508
  250.9 17.3 %all-to-all-start.8 = ((f32[4,1,128,4]{3,0,1,2:T(4,128)}), f32[4,1,128,4]{3,0,1,2:T(4,128)S(1)}, u32[]{:S(2)}, u32[]{:S(2)}) async-start(f32[4,1,128,4]{3,0,1,2:T(4,128)} %copy.671), calls=%async_computation.8 | async-start | bytes 524288 | tf_op jit(solution)/shard_map/all_to_all | solution.py:70
  275.7 17.6 %all-to-all-start.9 = ((f32[4,1,2,256]{0,2,1,3:T(2,128)}), f32[4,1,2,256]{0,2,1,3:T(2,128)S(1)}, u32[]{:S(2)}, u32[]{:S(2)}) async-start(f32[4,1,2,256]{0,2,1,3:T(2,128)} %copy.677), calls=%async_computation.9 | async-start | bytes 524288 | tf_op jit(solution)/shard_map/all_to_all | solution.py:66
  304.4 18.6 %copy-start.58 = (f32[1,4,1,2,257]{4,3,1,2,0:T(2,128)S(1)}, f32[1,4,1,2,257]{4,3,1,2,0:T(2,128)}, u32[]{:S(2)}) copy-start(f32[1,4,1,2,257]{4,3,1,2,0:T(2,128)} %copy-done.57) | copy-start | bytes 24676
  304.4 18.6 %copy-start.60 = (f32[1,4,1,2,257]{4,3,1,2,0:T(2,128)S(1)}, f32[1,4,1,2,257]{4,3,1,2,0:T(2,128)}, u32[]{:S(2)}) copy-start(f32[1,4,1,2,257]{4,3,1,2,0:T(2,128)} %copy-done.59) | copy-start | bytes 24676
  304.4 18.6 %copy-start.62 = (f32[1,4,1,2,257]{4,3,1,2,0:T(2,128)S(1)}, f32[1,4,1,2,257]{4,3,1,2,0:T(2,128)}, u32[]{:S(2)}) copy-start(f32[1,4,1,2,257]{4,3,1,2,0:T(2,128)} %copy-done.61) | copy-start | bytes 24676
  304.5 18.6 %copy-start.64 = (f32[1,4,1,2,257]{4,3,1,2,0:T(2,128)S(1)}, f32[1,4,1,2,257]{4,3,1,2,0:T(2,128)}, u32[]{:S(2)}) copy-start(f32[1,4,1,2,257]{4,3,1,2,0:T(2,128)} %copy-done.63) | copy-start | bytes 24676
  304.5 19.0 %copy-start.6 = (f32[514,128]{1,0:T(8,128)S(1)}, f32[514,128]{1,0:T(8,128)}, u32[]{:S(2)}) copy-start(f32[514,128]{1,0:T(8,128)} %copy-done.5) | copy-start | bytes 789508
  304.5 19.0 %copy-start.77 = (f32[2,4,128]{2,1,0:T(4,128)S(1)}, f32[2,4,128]{2,1,0:T(4,128)}, u32[]{:S(2)}) copy-start(f32[2,4,128]{2,1,0:T(4,128)} %param.26) | copy-start | bytes 12292
  305.3 18.8 %copy-start.19 = (f32[514,128]{1,0:T(8,128)S(1)}, f32[514,128]{1,0:T(8,128)}, u32[]{:S(2)}) copy-start(f32[514,128]{1,0:T(8,128)} %copy-done.18) | copy-start | bytes 789508
  305.4 17.3 %all-to-all-start.10 = ((f32[4,1,128,4]{3,0,1,2:T(4,128)}), f32[4,1,128,4]{3,0,1,2:T(4,128)S(1)}, u32[]{:S(2)}, u32[]{:S(2)}) async-start(f32[4,1,128,4]{3,0,1,2:T(4,128)} %copy.684), calls=%async_computation.10 | async-start | bytes 524288 | tf_op jit(solution)/shard_map/all_to_all | solution.py:70
  327.3 17.3 %all-to-all-start.11 = ((f32[4,1,2,256]{0,2,1,3:T(2,128)}), f32[4,1,2,256]{0,2,1,3:T(2,128)S(1)}, u32[]{:S(2)}, u32[]{:S(2)}) async-start(f32[4,1,2,256]{0,2,1,3:T(2,128)} %copy.690), calls=%async_computation.11 | async-start | bytes 524288 | tf_op jit(solution)/shard_map/all_to_all | solution.py:66
  350.7 18.5 %copy-start.50 = (f32[1,4,1,2,257]{4,3,1,2,0:T(2,128)S(1)}, f32[1,4,1,2,257]{4,3,1,2,0:T(2,128)}, u32[]{:S(2)}) copy-start(f32[1,4,1,2,257]{4,3,1,2,0:T(2,128)} %copy-done.49) | copy-start | bytes 24676
  350.7 18.5 %copy-start.52 = (f32[1,4,1,2,257]{4,3,1,2,0:T(2,128)S(1)}, f32[1,4,1,2,257]{4,3,1,2,0:T(2,128)}, u32[]{:S(2)}) copy-start(f32[1,4,1,2,257]{4,3,1,2,0:T(2,128)} %copy-done.51) | copy-start | bytes 24676
  350.8 19.0 %copy-start.2 = (f32[514,128]{1,0:T(8,128)S(1)}, f32[514,128]{1,0:T(8,128)}, u32[]{:S(2)}) copy-start(f32[514,128]{1,0:T(8,128)} %copy-done.1) | copy-start | bytes 789508
  351.7 18.8 %copy-start.15 = (f32[514,128]{1,0:T(8,128)S(1)}, f32[514,128]{1,0:T(8,128)}, u32[]{:S(2)}) copy-start(f32[514,128]{1,0:T(8,128)} %copy-done.14) | copy-start | bytes 789508
  351.7 17.3 %all-to-all-start.12 = ((f32[4,1,128,4]{3,0,1,2:T(4,128)}), f32[4,1,128,4]{3,0,1,2:T(4,128)S(1)}, u32[]{:S(2)}, u32[]{:S(2)}) async-start(f32[4,1,128,4]{3,0,1,2:T(4,128)} %copy.697), calls=%async_computation.12 | async-start | bytes 524288 | tf_op jit(solution)/shard_map/all_to_all | solution.py:70
  356.4 284.2 %all-reduce.50.cloned.1.call-start = ((), (), s32[]{:S(2)}) async-start(), calls=%async_computation.13 | async-start | bytes 262144 | tf_op jit(solution)/shard_map/psum | solution.py:135
  (83 other events, 296.6 us)
Sparse Core Ops, SparseCore 0:
  373.0 267.4 all-reduce.49
where the time goes:
time: 660 us; the launch traced here: 649 us
  waiting for transfers between devices  235 us (36%)
  blocking collectives  215 us (33%)
  local copies, waits for them, and re-layouts  70 us (11%)
  starting transfers between devices  50.5 us (8%)
  matrix products  39.1 us (6%)
  other arithmetic  22.5 us (3%)
  between operations  16.6 us (3%)
    psum x1, waiting for transfers between devices, on_device(): lax.psum((sums[0], sums[1], sums[2], sums[3], sums[4], sums[5]), ('band',...  162 us
    psum x1, blocking collectives, on_device(): lax.psum((sums[0], sums[1], sums[2], sums[3], sums[4], sums[5]), ('band',...  105 us
    all_to_all x3, blocking collectives, to_rows(): lax.all_to_all(field, 'band', split_axis=2, concat_axis=3, tiled=True)  55.7 us
    all_to_all x3, blocking collectives, to_columns(): lax.all_to_all(field, 'band', split_axis=3, concat_axis=2, tiled=True)  54.9 us
    all_to_all x3, waiting for transfers between devices, to_rows(): lax.all_to_all(field, 'band', split_axis=2, concat_axis=3, tiled=True)  35.5 us
    all_to_all x3, waiting for transfers between devices, to_columns(): lax.all_to_all(field, 'band', split_axis=3, concat_axis=2, tiled=True)  34.8 us
    all_to_all x3, starting transfers between devices, to_columns(): lax.all_to_all(field, 'band', split_axis=3, concat_axis=2, tiled=True)  18.9 us
    all_to_all x1, starting transfers between devices, on_device(): lax.all_to_all(stacked, 'band', split_axis=2, concat_axis=1, tiled=True)  17.3 us
  transfers between devices with their start and end apart: 8, of which 8 were waited for; matrix products, arithmetic and copies ran while one was open for 2% of the time, Pallas kernels for 0%

commit v1 on v0

--- a/solution.py
+++ b/solution.py
@@ -132,7 +132,7 @@
             )
         )
         sums = tuple((earlier + latest for earlier, latest in zip(sums, step_grads)))
-    sums = lax.psum((sums[0], sums[1], sums[2], sums[3], sums[4], sums[5]), ("band", "lev"))
+    sums = lax.psum(lax.psum((sums[0], sums[1], sums[2], sums[3], sums[4], sums[5]), "lev"), "band")
     return (field, sums[0], sums[1], sums[2], sums[3], sums[4], sums[5])
 
 

time: 660 us -> 765 us (1.16)
  the two profiles are of different devices: /device:TPU:1 before, /device:TPU:32 now
where the time goes in v1:
time: 765 us; the launch traced here: 754 us
  blocking collectives  414 us (54%)
  waiting for transfers between devices  122 us (16%)
  starting transfers between devices  71.7 us (9%)
  local copies, waits for them, and re-layouts  69.3 us (9%)
  matrix products  39.2 us (5%)
  other arithmetic  22.5 us (3%)
  between operations  16.6 us (2%)
    psum x1, blocking collectives, on_device(): lax.psum(lax.psum((sums[0], sums[1], sums[2], sums[3], sums[4], sums[5]),...  278 us
    psum x1, waiting for transfers between devices, on_device(): lax.psum((sums[0], sums[1], sums[2], sums[3], sums[4], sums[5]), 'lev')  66.2 us
    all_to_all x3, blocking collectives, to_columns(): lax.all_to_all(field, 'band', split_axis=3, concat_axis=2, tiled=True)  55.9 us
    all_to_all x3, blocking collectives, to_rows(): lax.all_to_all(field, 'band', split_axis=2, concat_axis=3, tiled=True)  55.6 us
    all_to_all x3, starting transfers between devices, to_columns(): lax.all_to_all(field, 'band', split_axis=3, concat_axis=2, tiled=True)  28.8 us
    all_to_all x3, waiting for transfers between devices, to_rows(): lax.all_to_all(field, 'band', split_axis=2, concat_axis=3, tiled=True)  26.7 us
    all_to_all x3, waiting for transfers between devices, to_columns(): lax.all_to_all(field, 'band', split_axis=3, concat_axis=2, tiled=True)  26.7 us
    all_to_all x3, starting transfers between devices, to_rows(): lax.all_to_all(field, 'band', split_axis=2, concat_axis=3, tiled=True)  26.4 us
  transfers between devices with their start and end apart: 9, of which 8 were waited for; matrix products, arithmetic and copies ran while one was open for 2% of the time, Pallas kernels for 0%

profile of v1, /device:TPU:32, one launch (start us, length us, event | category | flops | bytes accessed | tf_op | source)
XLA Modules:
  0.0 754.3 jit_solution(8531217500638710692)
XLA Ops:
  9.5 16.5 %all-to-all-start.1 = ((f32[2,2,256]{1,0,2:T(2,128)}), f32[2,2,256]{1,0,2:T(2,128)S(1)}, u32[]{:S(2)}, u32[]{:S(2)}) async-start(f32[2,2,256]{1,0,2:T(2,128)} %copy.634), calls=%async_computation.1 | async-start | bytes 524288 | tf_op jit(solution)/shard_map/all_to_all | solution.py:103
  35.0 1.9 all-to-all-done.1
  36.9 10.8 %all-to-all-start = ((f32[4,1,2,256]{0,2,1,3:T(2,128)}), f32[4,1,2,256]{0,2,1,3:T(2,128)S(1)}, u32[]{:S(2)}, u32[]{:S(2)}) async-start(f32[4,1,2,256]{0,2,1,3:T(2,128)} %copy.631), calls=%async_computation | async-start | bytes 524288 | tf_op jit(solution)/shard_map/all_to_all | solution.py:66
  49.5 8.8 %all-to-all-done = f32[4,1,2,256]{0,2,1,3:T(2,128)S(1)} async-done(((f32[4,1,2,256]{0,2,1,3:T(2,128)}), f32[4,1,2,256]{0,2,1,3:T(2,128)S(1)}, u32[]{:S(2)}, u32[]{:S(2)}) %all-to-all-start) | async-done | bytes 8224 | tf_op jit(solution)/shard_map/all_to_all | solution.py:66
  63.5 18.4 %all_to_all.231 = f32[4,1,128,4]{3,0,1,2:T(4,128)S(1)} all-to-all(f32[4,1,128,4]{3,0,1,2:T(4,128)S(1)} %copy.642), channel_id=1, replica_groups=mesh['band'=64,'lev'=8] {'band'}, dimensions={2} | all-to-all | bytes 16384 | tf_op jit(solution)/shard_map/all_to_all | solution.py:70
  86.0 18.4 %all_to_all.232 = f32[4,1,2,256]{0,2,1,3:T(2,128)S(1)} all-to-all(f32[4,1,2,256]{0,2,1,3:T(2,128)S(1)} %copy.646), channel_id=1, replica_groups=mesh['band'=64,'lev'=8] {'band'}, dimensions={3} | all-to-all | bytes 16384 | tf_op jit(solution)/shard_map/all_to_all | solution.py:66
  107.4 1.5 concatenate.121
  109.0 1.3 fusion.8
  114.4 18.4 %all_to_all.233 = f32[4,1,128,4]{3,0,1,2:T(4,128)S(1)} all-to-all(f32[4,1,128,4]{3,0,1,2:T(4,128)S(1)} %copy.651), channel_id=1, replica_groups=mesh['band'=64,'lev'=8] {'band'}, dimensions={2} | all-to-all | bytes 16384 | tf_op jit(solution)/shard_map/all_to_all | solution.py:70
  136.8 18.3 %all_to_all.234 = f32[4,1,2,256]{0,2,1,3:T(2,128)S(1)} all-to-all(f32[4,1,2,256]{0,2,1,3:T(2,128)S(1)} %copy.655), channel_id=1, replica_groups=mesh['band'=64,'lev'=8] {'band'}, dimensions={3} | all-to-all | bytes 16384 | tf_op jit(solution)/shard_map/all_to_all | solution.py:66
  157.8 1.5 slice_bitcast_fusion.15
  160.4 2.2 reshape.1580
  162.6 2.7 concatenate.123
  165.3 1.5 fusion.6
  171.1 1.6 mul.546
  172.7 1.9 multiply_reduce_fusion
  174.5 1.7 copy.716
  177.0 1.4 fusion.44
  178.4 1.6 copy.660
  179.9 18.8 %all_to_all.235 = f32[4,1,128,4]{3,0,1,2:T(4,128)S(1)} all-to-all(f32[4,1,128,4]{3,0,1,2:T(4,128)} %copy.660), channel_id=1, replica_groups=mesh['band'=64,'lev'=8] {'band'}, dimensions={2} | all-to-all | bytes 16384 | tf_op jit(solution)/shard_map/all_to_all | solution.py:70
  199.4 1.7 all_to_all.193
  202.5 1.6 copy.664
  204.0 19.2 %all_to_all.236 = f32[4,1,2,256]{0,2,1,3:T(2,128)} all-to-all(f32[4,1,2,256]{0,2,1,3:T(2,128)} %copy.664), channel_id=1, replica_groups=mesh['band'=64,'lev'=8] {'band'}, dimensions={3} | all-to-all | bytes 16384 | tf_op jit(solution)/shard_map/all_to_all | solution.py:66
  223.2 2.7 copy.711
  225.9 1.9 copy.666
  227.7 1.7 copy.667
  230.1 1.4 multiply_bitcast_fusion.2
  231.5 1.6 copy.669
  233.1 1.9 multiply_reduce_fusion.7
  235.7 1.7 reshape.1587
  237.4 1.6 fusion.90
  240.3 1.3 convolution_bitcast_fusion.4
  249.0 8.8 %all-to-all-start.8 = ((f32[4,1,128,4]{3,0,1,2:T(4,128)}), f32[4,1,128,4]{3,0,1,2:T(4,128)S(1)}, u32[]{:S(2)}, u32[]{:S(2)}) async-start(f32[4,1,128,4]{3,0,1,2:T(4,128)} %copy.671), calls=%async_computation.8 | async-start | bytes 524288 | tf_op jit(solution)/shard_map/all_to_all | solution.py:70
  257.7 1.5 convolution_bitcast_fusion.21
  259.3 8.1 %all-to-all-done.8 = f32[4,1,128,4]{3,0,1,2:T(4,128)S(1)} async-done(((f32[4,1,128,4]{3,0,1,2:T(4,128)}), f32[4,1,128,4]{3,0,1,2:T(4,128)S(1)}, u32[]{:S(2)}, u32[]{:S(2)}) %all-to-all-start.8) | async-done | bytes 8224 | tf_op jit(solution)/shard_map/all_to_all | solution.py:70
  269.9 1.3 convolution_bitcast_fusion.5
  274.9 9.0 %all-to-all-start.9 = ((f32[4,1,2,256]{0,2,1,3:T(2,128)}), f32[4,1,2,256]{0,2,1,3:T(2,128)S(1)}, u32[]{:S(2)}, u32[]{:S(2)}) async-start(f32[4,1,2,256]{0,2,1,3:T(2,128)} %copy.677), calls=%async_computation.9 | async-start | bytes 524288 | tf_op jit(solution)/shard_map/all_to_all | solution.py:66
  284.7 8.6 %all-to-all-done.9 = f32[4,1,2,256]{0,2,1,3:T(2,128)S(1)} async-done(((f32[4,1,2,256]{0,2,1,3:T(2,128)}), f32[4,1,2,256]{0,2,1,3:T(2,128)S(1)}, u32[]{:S(2)}, u32[]{:S(2)}) %all-to-all-start.9) | async-done | bytes 8224 | tf_op jit(solution)/shard_map/all_to_all | solution.py:66
  305.4 8.8 %all-to-all-start.10 = ((f32[4,1,128,4]{3,0,1,2:T(4,128)}), f32[4,1,128,4]{3,0,1,2:T(4,128)S(1)}, u32[]{:S(2)}, u32[]{:S(2)}) async-start(f32[4,1,128,4]{3,0,1,2:T(4,128)} %copy.684), calls=%async_computation.10 | async-start | bytes 524288 | tf_op jit(solution)/shard_map/all_to_all | solution.py:70
  314.4 9.3 %all-to-all-done.10 = f32[4,1,128,4]{3,0,1,2:T(4,128)S(1)} async-done(((f32[4,1,128,4]{3,0,1,2:T(4,128)}), f32[4,1,128,4]{3,0,1,2:T(4,128)S(1)}, u32[]{:S(2)}, u32[]{:S(2)}) %all-to-all-start.10) | async-done | bytes 8224 | tf_op jit(solution)/shard_map/all_to_all | solution.py:70
  328.4 9.0 %all-to-all-start.11 = ((f32[4,1,2,256]{0,2,1,3:T(2,128)}), f32[4,1,2,256]{0,2,1,3:T(2,128)S(1)}, u32[]{:S(2)}, u32[]{:S(2)}) async-start(f32[4,1,2,256]{0,2,1,3:T(2,128)} %copy.690), calls=%async_computation.11 | async-start | bytes 524288 | tf_op jit(solution)/shard_map/all_to_all | solution.py:66
  337.6 9.2 %all-to-all-done.11 = f32[4,1,2,256]{0,2,1,3:T(2,128)S(1)} async-done(((f32[4,1,2,256]{0,2,1,3:T(2,128)}), f32[4,1,2,256]{0,2,1,3:T(2,128)S(1)}, u32[]{:S(2)}, u32[]{:S(2)}) %all-to-all-start.11) | async-done | bytes 8224 | tf_op jit(solution)/shard_map/all_to_all | solution.py:66
  353.9 8.8 %all-to-all-start.12 = ((f32[4,1,128,4]{3,0,1,2:T(4,128)}), f32[4,1,128,4]{3,0,1,2:T(4,128)S(1)}, u32[]{:S(2)}, u32[]{:S(2)}) async-start(f32[4,1,128,4]{3,0,1,2:T(4,128)} %copy.697), calls=%async_computation.12 | async-start | bytes 524288 | tf_op jit(solution)/shard_map/all_to_all | solution.py:70
  363.1 9.3 %all-to-all-done.12 = f32[4,1,128,4]{3,0,1,2:T(4,128)S(1)} async-done(((f32[4,1,128,4]{3,0,1,2:T(4,128)}), f32[4,1,128,4]{3,0,1,2:T(4,128)S(1)}, u32[]{:S(2)}, u32[]{:S(2)}) %all-to-all-start.12) | async-done | bytes 8224 | tf_op jit(solution)/shard_map/all_to_all | solution.py:70
  376.8 66.2 %all-reduce.52.cloned.1.call-done = f32[2,128,128]{2,1,0:T(8,128)} async-done(((f32[2,128,128]{2,1,0:T(8,128)}), f32[2,128,128]{2,1,0:T(8,128)}) %all-reduce.52.cloned.1.call-update) | async-done | bytes 131088 | tf_op jit(solution)/shard_map/psum | solution.py:135
  443.0 24.4 %all-reduce.48 = (f32[2,20,128]{2,1,0:T(8,128)S(1)}, f32[2,128]{1,0:T(2,128)S(1)}, f32[2,128]{1,0:T(2,128)S(1)}, f32[2,4,128]{2,1,0:T(4,128)S(1)}, f32[2,4]{1,0:T(2,128)S(1)}) all-reduce(f32[2,20,128]{2,1,0:T(8,128)S(1)} %fusion.37, f32[2,128]{1,0:T(2,128)S(1)} %get-tuple-element.221, ...), channel_id=1, replica_groups=mesh['band'=64,'lev'=8] {'lev'}, use_global_device_ids=true, to_apply=%region_24.25 | all-reduce | flops 6664 | bytes 53312 | tf_op jit(solution)/shard_map/psum | solution.py:135
  467.5 277.7 %all-reduce.47 = (f32[2,20,128]{2,1,0:T(8,128)S(1)}, f32[2,128]{1,0:T(2,128)}, f32[2,128]{1,0:T(2,128)}, f32[2,4,128]{2,1,0:T(4,128)}, f32[2,4]{1,0:T(2,128)}) all-reduce(f32[2,20,128]{2,1,0:T(8,128)S(1)} %get-tuple-element.101, f32[2,128]{1,0:T(2,128)S(1)} %get-tuple-element.102, ...), channel_id=1, replica_groups=mesh['band'=64,'lev'=8] {'band'}, use_global_device_ids=true, to_apply=%region_25.26 | all-reduce | flops 6664 | bytes 53312 | tf_op jit(solution)/shard_map/psum | solution.py:135
  745.7 1.6 copy.765
  (497 shorter events, 88.8 us)
Async XLA Ops:
  7.2 25.7 %copy-start = (f32[2,128,128]{2,1,0:T(8,128)S(1)}, f32[2,128,128]{2,1,0:T(8,128)}, u32[]{:S(2)}) copy-start(f32[2,128,128]{2,1,0:T(8,128)} %param.24) | copy-start | bytes 393220
  8.6 24.9 %copy-start.73 = (f32[2,4,128]{2,1,0:T(4,128)S(1)}, f32[2,4,128]{2,1,0:T(4,128)}, u32[]{:S(2)}) copy-start(f32[2,4,128]{2,1,0:T(4,128)} %param.26) | copy-start | bytes 12292
  9.5 24.4 %copy-start.100 = (f32[4]{0:T(128)S(1)}, f32[4]{0:T(128)}, u32[]{:S(2)}) copy-start(f32[4]{0:T(128)} %constant.29.clone) | copy-start | bytes 52
  9.5 24.6 %copy-start.82 = (f32[4,1,2,256]{3,2,1,0:T(2,128)S(1)}, f32[4,1,2,256]{3,2,1,0:T(2,128)}, u32[]{:S(2)}) copy-start(f32[4,1,2,256]{3,2,1,0:T(2,128)} %param.17) | copy-start | bytes 24580
  9.5 27.5 %all-to-all-start.1 = ((f32[2,2,256]{1,0,2:T(2,128)}), f32[2,2,256]{1,0,2:T(2,128)S(1)}, u32[]{:S(2)}, u32[]{:S(2)}) async-start(f32[2,2,256]{1,0,2:T(2,128)} %copy.634), calls=%async_computation.1 | async-start | bytes 524288 | tf_op jit(solution)/shard_map/all_to_all | solution.py:103
  28.3 31.9 %copy-start.103 = (f32[128]{0:T(128)}, f32[128]{0:T(128)S(1)}, u32[]{:S(2)}) copy-start(f32[128]{0:T(128)S(1)} %get-tuple-element.183) | copy-start | bytes 1540
  28.3 54.2 %copy-start.105 = (f32[128]{0:T(128)}, f32[128]{0:T(128)S(1)}, u32[]{:S(2)}) copy-start(f32[128]{0:T(128)S(1)} %get-tuple-element.184) | copy-start | bytes 1540
  29.1 31.8 %copy-start.111 = (f32[128]{0:T(128)}, f32[128]{0:T(128)S(1)}, u32[]{:S(2)}) copy-start(f32[128]{0:T(128)S(1)} %get-tuple-element.181) | copy-start | bytes 1540
  29.1 54.2 %copy-start.112 = (f32[128]{0:T(128)}, f32[128]{0:T(128)S(1)}, u32[]{:S(2)}) copy-start(f32[128]{0:T(128)S(1)} %get-tuple-element.182) | copy-start | bytes 1540
  29.9 31.7 %copy-start.104 = (f32[4]{0:T(128)}, f32[4]{0:T(128)S(1)}, u32[]{:S(2)}) copy-start(f32[4]{0:T(128)S(1)} %get-tuple-element.179) | copy-start | bytes 52
  29.9 54.0 %copy-start.107 = (f32[4]{0:T(128)}, f32[4]{0:T(128)S(1)}, u32[]{:S(2)}) copy-start(f32[4]{0:T(128)S(1)} %get-tuple-element.180) | copy-start | bytes 52
  29.9 52.6 %copy-start.91 = (f32[1,514]{1,0:T(1,128)}, f32[1,514]{1,0:T(1,128)S(1)}, u32[]{:S(2)}) copy-start(f32[1,514]{1,0:T(1,128)S(1)} %reshape.1571) | copy-start | bytes 6172
  30.0 52.5 %copy-start.93 = (f32[1,514]{1,0:T(1,128)}, f32[1,514]{1,0:T(1,128)S(1)}, u32[]{:S(2)}) copy-start(f32[1,514]{1,0:T(1,128)S(1)} %reshape.1570) | copy-start | bytes 6172
  30.9 51.5 %copy-start.95 = (f32[1,514]{1,0:T(1,128)}, f32[1,514]{1,0:T(1,128)S(1)}, u32[]{:S(2)}) copy-start(f32[1,514]{1,0:T(1,128)S(1)} %reshape.1569) | copy-start | bytes 6172
  31.0 51.5 %copy-start.97 = (f32[1,514]{1,0:T(1,128)}, f32[1,514]{1,0:T(1,128)S(1)}, u32[]{:S(2)}) copy-start(f32[1,514]{1,0:T(1,128)S(1)} %reshape.1568) | copy-start | bytes 6172
  31.9 50.7 %copy-start.43 = (f32[1,20,128]{2,0,1:T(1,128)}, f32[1,20,128]{2,0,1:T(1,128)S(1)}, u32[]{:S(2)}) copy-start(f32[1,20,128]{2,0,1:T(1,128)S(1)} %get-tuple-element.159) | copy-start | bytes 30724
  36.9 21.3 %all-to-all-start = ((f32[4,1,2,256]{0,2,1,3:T(2,128)}), f32[4,1,2,256]{0,2,1,3:T(2,128)S(1)}, u32[]{:S(2)}, u32[]{:S(2)}) async-start(f32[4,1,2,256]{0,2,1,3:T(2,128)} %copy.631), calls=%async_computation | async-start | bytes 524288 | tf_op jit(solution)/shard_map/all_to_all | solution.py:66
  114.2 19.9 %copy-start.113 = (f32[128]{0:T(128)S(1)}, f32[128]{0:T(128)}, u32[]{:S(2)}) copy-start(f32[128]{0:T(128)} %copy-done.112) | copy-start | bytes 1540
  248.0 19.7 %copy-start.66 = (f32[1,4,1,2,257]{4,3,1,2,0:T(2,128)S(1)}, f32[1,4,1,2,257]{4,3,1,2,0:T(2,128)}, u32[]{:S(2)}) copy-start(f32[1,4,1,2,257]{4,3,1,2,0:T(2,128)} %copy-done.65) | copy-start | bytes 24676
  248.0 19.7 %copy-start.68 = (f32[1,4,1,2,257]{4,3,1,2,0:T(2,128)S(1)}, f32[1,4,1,2,257]{4,3,1,2,0:T(2,128)}, u32[]{:S(2)}) copy-start(f32[1,4,1,2,257]{4,3,1,2,0:T(2,128)} %copy-done.67) | copy-start | bytes 24676
  248.0 19.7 %copy-start.70 = (f32[1,4,1,2,257]{4,3,1,2,0:T(2,128)S(1)}, f32[1,4,1,2,257]{4,3,1,2,0:T(2,128)}, u32[]{:S(2)}) copy-start(f32[1,4,1,2,257]{4,3,1,2,0:T(2,128)} %copy-done.69) | copy-start | bytes 24676
  248.0 19.7 %copy-start.72 = (f32[1,4,1,2,257]{4,3,1,2,0:T(2,128)S(1)}, f32[1,4,1,2,257]{4,3,1,2,0:T(2,128)}, u32[]{:S(2)}) copy-start(f32[1,4,1,2,257]{4,3,1,2,0:T(2,128)} %copy-done.71) | copy-start | bytes 24676
  248.0 20.7 %copy-start.10 = (f32[514,128]{1,0:T(8,128)S(1)}, f32[514,128]{1,0:T(8,128)}, u32[]{:S(2)}) copy-start(f32[514,128]{1,0:T(8,128)} %copy-done.9) | copy-start | bytes 789508
  248.1 20.7 %copy-start.76 = (f32[2,4,128]{2,1,0:T(4,128)S(1)}, f32[2,4,128]{2,1,0:T(4,128)}, u32[]{:S(2)}) copy-start(f32[2,4,128]{2,1,0:T(4,128)} %param.26) | copy-start | bytes 12292
  248.9 21.0 %copy-start.23 = (f32[514,128]{1,0:T(8,128)S(1)}, f32[514,128]{1,0:T(8,128)}, u32[]{:S(2)}) copy-start(f32[514,128]{1,0:T(8,128)} %copy-done.22) | copy-start | bytes 789508
  249.0 18.4 %all-to-all-start.8 = ((f32[4,1,128,4]{3,0,1,2:T(4,128)}), f32[4,1,128,4]{3,0,1,2:T(4,128)S(1)}, u32[]{:S(2)}, u32[]{:S(2)}) async-start(f32[4,1,128,4]{3,0,1,2:T(4,128)} %copy.671), calls=%async_computation.8 | async-start | bytes 524288 | tf_op jit(solution)/shard_map/all_to_all | solution.py:70
  274.9 18.5 %all-to-all-start.9 = ((f32[4,1,2,256]{0,2,1,3:T(2,128)}), f32[4,1,2,256]{0,2,1,3:T(2,128)S(1)}, u32[]{:S(2)}, u32[]{:S(2)}) async-start(f32[4,1,2,256]{0,2,1,3:T(2,128)} %copy.677), calls=%async_computation.9 | async-start | bytes 524288 | tf_op jit(solution)/shard_map/all_to_all | solution.py:66
  304.4 19.7 %copy-start.58 = (f32[1,4,1,2,257]{4,3,1,2,0:T(2,128)S(1)}, f32[1,4,1,2,257]{4,3,1,2,0:T(2,128)}, u32[]{:S(2)}) copy-start(f32[1,4,1,2,257]{4,3,1,2,0:T(2,128)} %copy-done.57) | copy-start | bytes 24676
  304.4 19.7 %copy-start.60 = (f32[1,4,1,2,257]{4,3,1,2,0:T(2,128)S(1)}, f32[1,4,1,2,257]{4,3,1,2,0:T(2,128)}, u32[]{:S(2)}) copy-start(f32[1,4,1,2,257]{4,3,1,2,0:T(2,128)} %copy-done.59) | copy-start | bytes 24676
  304.4 19.7 %copy-start.62 = (f32[1,4,1,2,257]{4,3,1,2,0:T(2,128)S(1)}, f32[1,4,1,2,257]{4,3,1,2,0:T(2,128)}, u32[]{:S(2)}) copy-start(f32[1,4,1,2,257]{4,3,1,2,0:T(2,128)} %copy-done.61) | copy-start | bytes 24676
  304.5 19.7 %copy-start.64 = (f32[1,4,1,2,257]{4,3,1,2,0:T(2,128)S(1)}, f32[1,4,1,2,257]{4,3,1,2,0:T(2,128)}, u32[]{:S(2)}) copy-start(f32[1,4,1,2,257]{4,3,1,2,0:T(2,128)} %copy-done.63) | copy-start | bytes 24676
  304.5 20.1 %copy-start.6 = (f32[514,128]{1,0:T(8,128)S(1)}, f32[514,128]{1,0:T(8,128)}, u32[]{:S(2)}) copy-start(f32[514,128]{1,0:T(8,128)} %copy-done.5) | copy-start | bytes 789508
  304.5 20.1 %copy-start.77 = (f32[2,4,128]{2,1,0:T(4,128)S(1)}, f32[2,4,128]{2,1,0:T(4,128)}, u32[]{:S(2)}) copy-start(f32[2,4,128]{2,1,0:T(4,128)} %param.26) | copy-start | bytes 12292
  305.4 19.9 %copy-start.19 = (f32[514,128]{1,0:T(8,128)S(1)}, f32[514,128]{1,0:T(8,128)}, u32[]{:S(2)}) copy-start(f32[514,128]{1,0:T(8,128)} %copy-done.18) | copy-start | bytes 789508
  305.4 18.4 %all-to-all-start.10 = ((f32[4,1,128,4]{3,0,1,2:T(4,128)}), f32[4,1,128,4]{3,0,1,2:T(4,128)S(1)}, u32[]{:S(2)}, u32[]{:S(2)}) async-start(f32[4,1,128,4]{3,0,1,2:T(4,128)} %copy.684), calls=%async_computation.10 | async-start | bytes 524288 | tf_op jit(solution)/shard_map/all_to_all | solution.py:70
  328.4 18.4 %all-to-all-start.11 = ((f32[4,1,2,256]{0,2,1,3:T(2,128)}), f32[4,1,2,256]{0,2,1,3:T(2,128)S(1)}, u32[]{:S(2)}, u32[]{:S(2)}) async-start(f32[4,1,2,256]{0,2,1,3:T(2,128)} %copy.690), calls=%async_computation.11 | async-start | bytes 524288 | tf_op jit(solution)/shard_map/all_to_all | solution.py:66
  353.0 19.7 %copy-start.50 = (f32[1,4,1,2,257]{4,3,1,2,0:T(2,128)S(1)}, f32[1,4,1,2,257]{4,3,1,2,0:T(2,128)}, u32[]{:S(2)}) copy-start(f32[1,4,1,2,257]{4,3,1,2,0:T(2,128)} %copy-done.49) | copy-start | bytes 24676
  353.0 19.7 %copy-start.52 = (f32[1,4,1,2,257]{4,3,1,2,0:T(2,128)S(1)}, f32[1,4,1,2,257]{4,3,1,2,0:T(2,128)}, u32[]{:S(2)}) copy-start(f32[1,4,1,2,257]{4,3,1,2,0:T(2,128)} %copy-done.51) | copy-start | bytes 24676
  353.0 19.7 %copy-start.54 = (f32[1,4,1,2,257]{4,3,1,2,0:T(2,128)S(1)}, f32[1,4,1,2,257]{4,3,1,2,0:T(2,128)}, u32[]{:S(2)}) copy-start(f32[1,4,1,2,257]{4,3,1,2,0:T(2,128)} %copy-done.53) | copy-start | bytes 24676
  353.0 19.7 %copy-start.56 = (f32[1,4,1,2,257]{4,3,1,2,0:T(2,128)S(1)}, f32[1,4,1,2,257]{4,3,1,2,0:T(2,128)}, u32[]{:S(2)}) copy-start(f32[1,4,1,2,257]{4,3,1,2,0:T(2,128)} %copy-done.55) | copy-start | bytes 24676
  353.0 20.1 %copy-start.2 = (f32[514,128]{1,0:T(8,128)S(1)}, f32[514,128]{1,0:T(8,128)}, u32[]{:S(2)}) copy-start(f32[514,128]{1,0:T(8,128)} %copy-done.1) | copy-start | bytes 789508
  353.9 19.9 %copy-start.15 = (f32[514,128]{1,0:T(8,128)S(1)}, f32[514,128]{1,0:T(8,128)}, u32[]{:S(2)}) copy-start(f32[514,128]{1,0:T(8,128)} %copy-done.14) | copy-start | bytes 789508
  353.9 18.4 %all-to-all-start.12 = ((f32[4,1,128,4]{3,0,1,2:T(4,128)}), f32[4,1,128,4]{3,0,1,2:T(4,128)S(1)}, u32[]{:S(2)}, u32[]{:S(2)}) async-start(f32[4,1,128,4]{3,0,1,2:T(4,128)} %copy.697), calls=%async_computation.12 | async-start | bytes 524288 | tf_op jit(solution)/shard_map/all_to_all | solution.py:70
  362.8 80.2 %all-reduce.52.cloned.1.call-start = ((), (), s32[]{:S(2)}) async-start(), calls=%async_computation.13 | async-start | bytes 262144 | tf_op jit(solution)/shard_map/psum | solution.py:135
  374.7 68.3 %copy-start.120 = (f32[4]{0:T(128)S(1)}, f32[4]{0:T(128)}, u32[]{:S(2)}) copy-start(f32[4]{0:T(128)} %get-tuple-element.114) | copy-start | bytes 52
  374.7 68.3 %copy-start.121 = (f32[4]{0:T(128)S(1)}, f32[4]{0:T(128)}, u32[]{:S(2)}) copy-start(f32[4]{0:T(128)} %get-tuple-element.116) | copy-start | bytes 52
  374.7 68.3 %copy-start.122 = (f32[4]{0:T(128)S(1)}, f32[4]{0:T(128)}, u32[]{:S(2)}) copy-start(f32[4]{0:T(128)} %get-tuple-element.112) | copy-start | bytes 52
  376.3 369.4 %all-reduce.54.cloned.1.call-start = ((), (), s32[]{:S(2)}) async-start(), calls=%async_computation.14 | async-start | bytes 262144 | tf_op jit(solution)/shard_map/psum | solution.py:135
  (84 other events, 397.1 us)
Sparse Core Ops, SparseCore 0:
  376.5 66.4 all-reduce.51
  446.2 150.0 all-reduce.53
